TPU v7x, 32 devices: a whole 2x2x4 slice. The times are simulated.
32 devices in a mesh: rows: 8 (over z, y), cols: 4 (over x, core).
Axes of the slice: x: 2, y: 2, z: 4, core: 2. Of those that a mesh axis runs over, the one named last changes fastest.
Arguments:
- right_sample: bfloat16 [2048, 320], P('rows', 'cols'), may hold values from -6 to 6
- left_sample: bfloat16 [2048, 320], P('rows', 'cols'), may hold values from -6 to 6
- updates: bfloat16 [8, 512, 512], P('rows'), may hold values from -0.25 to 0.25
- pattern: int32 [8, 4, 4], P('rows'), may hold values 0 or 1
- targets: int32 [8, 512], P('rows'), may hold values from 0 to 2047, as said below
- cluster_pos: int32 [2048], P('rows'), may hold values from 0 to 2047, as said below
- pivots: int32 [8, 128], P('rows'), may hold values from 0 to 255, as said below
Outputs:
- forward_out: float32 [2048, 320], P('rows', 'cols')
- transposed_out: float32 [2048, 320], P('rows', 'cols')
- interp: float32 [2048, 128], P('rows')
Inputs may be any that keep to these rules, and one draw needn't show every extreme that they name: `targets`: the tile rows of one index of rows name at most 96 front rows held by any one index of rows; in every draw one index of rows receives exactly 96 from every index of rows. `cluster_pos`: A permutation; the 256 front rows of one index of rows take exactly 32 positions in the block of every index of rows. The pivots of one leaf are distinct.
All inputs are finite; a program needn't handle non-finite values. No bound on the sum of `pattern` on one device may be relied on, other than what follows from the above.
Results may differ from a plain program's by a relative error of at most 0.0003.
Values may be sent and summed in bfloat16 or wider, within the bound.
A program may use at most 64 MiB of HBM per device.

v0:
```python
import functools

import jax
import jax.numpy as jnp
from jax import lax
from jax.experimental import pallas as pl
from jax.experimental.pallas import tpu as pltpu
from jax.sharding import PartitionSpec as P

K = 320
LEAF = 256
RANK = 128
MESH = pl.DeviceIdType.MESH
F32 = jnp.float32
BF16 = jnp.bfloat16
QMAX = 32766.0
STEP = 4


def _up(value, unit):
    return -(-value // unit) * unit


def _dot(a, b, dims=((1,), (0,))):
    return lax.dot_general(a, b, (dims, ((), ())), preferred_element_type=F32)


TN = ((0,), (0,))
NT = ((1,), (1,))


def _iota(shape, dim):
    return lax.broadcasted_iota(jnp.int32, shape, dim)


def _split2(x):
    hi = x.astype(BF16)
    return hi, (x - hi.astype(F32)).astype(BF16)


def _digits(q):
    hi = jnp.floor(q * (1.0 / 256.0))
    return hi.astype(BF16), (q - 256.0 * hi).astype(BF16)


def _move_exact(sel, hi, lo, dims=((1,), (0,))):
    return 256.0 * _dot(sel, hi, dims) + _dot(sel, lo, dims)


def _encode(x, width):
    lane = _iota(x.shape, 1)
    top = jnp.max(jnp.where(lane < width, jnp.abs(x), 0.0), axis=1, keepdims=True)
    expo = jnp.clip(
        jnp.ceil(jnp.log(jnp.maximum(top, 1e-30)) * 1.4426950408889634 + 0.001), -96.0, 120.0
    )
    code = jnp.floor(x * (QMAX / jnp.exp2(expo)) + 0.5)
    return jnp.where(lane < width, code, jnp.where(lane == width, expo, 0.0))


def _decode(q, width):
    lane = _iota(q.shape, 1)
    scale = jnp.exp2(q[:, width : width + 1]) * (1.0 / QMAX)
    return jnp.where(lane < width, q * scale, 0.0)


def _code_rows(x):
    top = jnp.max(jnp.abs(x), axis=0, keepdims=True)
    expo = jnp.clip(
        jnp.ceil(jnp.log(jnp.maximum(top, 1e-30)) * 1.4426950408889634 + 0.001), -96.0, 120.0
    )
    return expo, jnp.floor(x * (QMAX / jnp.exp2(expo)) + 0.5)


def _encode_part(part, pickt):
    on = pickt.astype(F32) > 0.5
    expo, code = _code_rows(jnp.where(on, 0.0, part))
    own_expo, own_code = _code_rows(jnp.sum(jnp.where(on, part, 0.0), axis=0, keepdims=True))
    row = _iota((16, part.shape[1]), 0)
    tail = jnp.where(row == 0, expo, jnp.where(row == 1, own_expo, jnp.where(row == 2, own_code, 0.0)))
    return jnp.concatenate([code, tail], axis=0).astype(jnp.int32).astype(jnp.int16)


def _folds(rows, lanes, width):
    stride = width + 2 - (lanes - 128)
    return max(f for f in range(1, 9)
               if f == 1 or (rows % f == 0 and (rows // f) % 16 == 0 and f * stride <= 128))


def _packed(rows, lanes, width):
    return rows * (lanes // 128 - 1) + rows // _folds(rows, lanes, width)


def _pack(x, width):
    rows, lanes = x.shape
    folds = _folds(rows, lanes, width)
    stride = width + 2 - (lanes - 128)
    part = rows // folds
    last = x[:, lanes - 128 :]
    tail = last[:part]
    for g in range(1, folds):
        tail = tail + pltpu.roll(last[g * part : (g + 1) * part], g * stride, axis=1)
    return jnp.concatenate([x[:, i : i + 128] for i in range(0, lanes - 128, 128)] + [tail], axis=0)


def _unpack(y, rows, lanes, width):
    folds = _folds(rows, lanes, width)
    stride = width + 2 - (lanes - 128)
    panels = lanes // 128 - 1
    tail = y[panels * rows :]
    pieces = [tail] + [pltpu.roll(tail, 128 - g * stride, axis=1) for g in range(1, folds)]
    last = jnp.concatenate(pieces, axis=0) if folds > 1 else tail
    last = jnp.where(_iota(last.shape, 1) < stride, last, 0.0)
    return jnp.concatenate([y[i * rows : (i + 1) * rows] for i in range(panels)] + [last], axis=1)


def _positions(row, count, span, stride):
    length = row.shape[1]
    rows8 = _up(count, 16)
    holder = _iota((rows8, length), 0)
    hot = (row >= holder * span) & (row < (holder + 1) * span)
    hot_f = hot.astype(F32)
    before = (_iota((length, length), 0) < _iota((length, length), 1)).astype(F32).astype(BF16)
    rank = _dot(hot_f.astype(BF16), before)
    slot = jnp.sum(hot_f * (rank + (holder * stride).astype(F32)), axis=0, keepdims=True)
    base = jnp.sum(hot_f * (holder * span).astype(F32), axis=0, keepdims=True)
    return slot.astype(jnp.int32), row - base.astype(jnp.int32)


def _order(count):
    return sorted(range(1, count), key=lambda o: (min(o, count - o), o))


def _each(count, body, far=False):
    if count <= 17:
        for o in _order(count)[:: -1 if far else 1]:
            body(o)
    else:
        lax.fori_loop(1, count, lambda o, c: (body(o), c)[1], jnp.int32(0))


def moving_kernel(
    n, ncols, width, cap, group,
    right_ref, left_ref, updates_ref, pattern_ref, targets_ref, pos_ref, pivots_ref,
    parts_ref, own_ref, pickt_ref,
    both_ref, req_out, req_in, hot_ref, pick_out, pick_in, gather_ref, sel_ref, selt_ref, masked_ref, masked_t_ref, con_out, con_in, mov_out, mov_in, part_own,
    s0, r0, s1, r1, s2, r2, s3, r3, s4, r4,
):
    me = lax.axis_index("rows")
    mycol = lax.axis_index("cols")
    rows_loc, lanes = both_ref.shape
    total = targets_ref.shape[1]
    children, block, _ = updates_ref.shape
    tiles = pattern_ref.shape[1]
    tile = block // tiles

    def to_row(o):
        return lax.rem(me + o, n)

    def from_row(o):
        return lax.rem(me - o + n, n)

    barrier = pltpu.get_barrier_semaphore()
    _each(n, lambda o: pl.semaphore_signal(
        barrier, inc=1, device_id={"rows": to_row(o)}, device_id_type=MESH))
    for o in range(1, ncols):
        pl.semaphore_signal(
            barrier, inc=1, device_id={"cols": lax.rem(mycol + o, ncols)}, device_id_type=MESH)

    def copy(out, into, send, recv, o):
        return pltpu.make_async_remote_copy(
            src_ref=out.at[to_row(o)], dst_ref=into.at[me], send_sem=send.at[o],
            recv_sem=recv.at[o], device_id={"rows": to_row(o)}, device_id_type=MESH)

    def arrival(out, into, send, recv, o):
        return pltpu.make_async_remote_copy(
            src_ref=out.at[to_row(o)], dst_ref=into.at[from_row(o)], send_sem=send.at[o],
            recv_sem=recv.at[o], device_id={"rows": to_row(o)}, device_id_type=MESH)

    half = width // 2
    sides = ((right_ref, 0), (left_ref, half))
    slot, local = _positions(targets_ref[...], n, rows_loc, cap)
    digits = jnp.where(
        _iota((16, total), 0) < 8, jnp.bitwise_and(local, 255), jnp.right_shift(local, 8))
    digits = digits.astype(F32).astype(BF16)

    def make_request(d, where):
        part = (_iota((cap, total), 0) + d * cap == slot).astype(F32).astype(BF16)
        sel_ref[pl.ds(pl.multiple_of(d * cap, 16), cap), :] = part
        ask = _dot(digits, part, NT)
        where[d, :, :cap] = (ask[:1] + 256.0 * ask[8:9]).astype(jnp.int32)

    _each(n, lambda o: make_request(to_row(o), req_out), far=True)
    pl.semaphore_wait(barrier, n - 1 + ncols - 1)
    _each(n, lambda o: copy(req_out, req_in, s0, r0, o).start(), far=True)
    make_request(me, req_in)
    chosen = _iota((rows_loc, RANK), 0) == pivots_ref[...]
    pickt_ref[...] = jnp.transpose(chosen.astype(F32)).astype(BF16)

    both_ref[...] = functools.reduce(jnp.add, [
        _dot(ref[...],
             (_iota((half, lanes), 1) == _iota((half, lanes), 0) + at).astype(F32).astype(BF16), TN)
        for ref, at in sides]).astype(BF16)
    same = _iota((total, total), 0) == _iota((total, total), 1)
    slot_col = jnp.sum(jnp.where(same, slot.astype(F32), 0.0), axis=1, keepdims=True)
    slot_col = slot_col.astype(jnp.int32)

    def make_selt(d):
        at = _iota((total, cap), 1) + d * cap
        selt_ref[d] = (at == slot_col).astype(F32).astype(BF16)

    make_selt(0)
    _each(n, make_selt)
    for c in range(children):
        for a in range(tiles):
            for b in range(tiles):
                part = updates_ref[c, a * tile : (a + 1) * tile, b * tile : (b + 1) * tile]
                keep = jnp.broadcast_to(pattern_ref[c, a, b], part.shape) != 0
                part = jnp.where(keep, part.astype(F32), 0.0)
                masked_ref[c, a * tile : (a + 1) * tile, b * tile : (b + 1) * tile] = part.astype(BF16)
                masked_t_ref[c, b * tile : (b + 1) * tile, a * tile : (a + 1) * tile] = (
                    jnp.transpose(part).astype(BF16))

    def make_pick(s, where):
        wanted = req_in[s][:, :cap]
        hot = (_iota((rows_loc, cap), 0) == wanted).astype(F32).astype(BF16)
        hot_ref[s] = hot
        where[s] = _pack(_dot(hot, both_ref[...], TN), width).astype(BF16)

    def answer(o):
        arrival(req_out, req_in, s0, r0, n - o).wait_recv()
        make_pick(to_row(o), pick_out)
        copy(pick_out, pick_in, s1, r1, o).start()

    _each(n, answer)
    def fetched(s):
        rows = _unpack(pick_in[s].astype(F32), cap, lanes, width).astype(BF16)
        return _dot(selt_ref[s], rows)

    make_pick(me, pick_in)
    gather_ref[...] = fetched(me)

    def take_rows(o):
        arrival(pick_out, pick_in, s1, r1, o).wait_recv()
        gather_ref[...] += fetched(from_row(o))

    _each(n, take_rows)
    gathered = gather_ref[...].astype(BF16)

    parts = []
    for c in range(children):
        some = gathered[c * block : (c + 1) * block]
        fwd = _dot(masked_ref[c], some)
        trn = _dot(masked_t_ref[c], some)
        parts.append(jnp.where(_iota(fwd.shape, 1) < width // 2, fwd, trn))
    contrib = parts[0] if children == 1 else jnp.concatenate(parts, axis=0)
    code_hi, code_lo = _digits(_encode(contrib, width))

    def make_con(d, where):
        part = sel_ref[pl.ds(pl.multiple_of(d * cap, 16), cap), :]
        moved = _pack(_move_exact(part, code_hi, code_lo), width)
        where[d] = moved.astype(jnp.int32).astype(jnp.int16)

    def send_con(o):
        make_con(to_row(o), con_out)
        copy(con_out, con_in, s2, r2, o).start()

    _each(n, send_con, far=True)
    make_con(me, con_in)

    slot2, place = _positions(pos_ref[...], n, rows_loc, group)
    sel2 = (_iota((n * group, rows_loc), 0) == slot2).astype(F32).astype(BF16)
    diag = _iota((rows_loc, rows_loc), 0) == _iota((rows_loc, rows_loc), 1)
    place_col = jnp.sum(jnp.where(diag, place.astype(F32) + 1.0, 0.0), axis=1, keepdims=True)

    def add_from(s, front):
        code = _unpack(con_in[s].astype(jnp.int32).astype(F32), cap, lanes, width)
        hi, lo = _split2(_decode(code, width))
        hot = hot_ref[s]
        return front + _dot(hot, hi) + _dot(hot, lo)

    front = add_from(me, jnp.zeros((rows_loc, lanes), F32))

    def take(o, front):
        arrival(con_out, con_in, s2, r2, o).wait_recv()
        return add_from(from_row(o), front)

    if n <= 17:
        for o in _order(n):
            front = take(o, front)
    else:
        front = lax.fori_loop(1, n, take, front)

    code = jnp.where(_iota(front.shape, 1) == width + 1, place_col, _encode(front, width))
    moved = _move_exact(sel2, *_digits(code))
    for d in range(n):
        block_d = _pack(moved[d * group : (d + 1) * group], width)
        mov_out[d] = block_d.astype(jnp.int32).astype(jnp.int16)

    def send_moved(o):
        copy(mov_out, mov_in, s3, r3, o).start()

    _each(n, send_moved, far=True)
    mov_in[me] = mov_out[me]
    _each(n, lambda o: arrival(mov_out, mov_in, s3, r3, o).wait_recv())
    got = jnp.concatenate(
        [_unpack(mov_in[d].astype(jnp.int32).astype(F32), group, lanes, width) for d in range(n)],
        axis=0)
    landing = got[:, width + 1 : width + 2].astype(jnp.int32) - 1
    hot2 = (_iota((n * group, rows_loc), 1) == landing).astype(F32).astype(BF16)
    coded = _move_exact(hot2, *_digits(got), TN)
    values = _decode(coded, width)
    hi, lo = _split2(values)
    pickt = pickt_ref[...]
    shi = _dot(pickt, hi).astype(BF16)
    slo = _dot(pickt, lo).astype(BF16)
    part = _dot(shi, hi, NT) + (_dot(shi, lo, NT) + _dot(slo, hi, NT))
    part_own[...] = _encode_part(part * (1.0 / (2.0 * K)), pickt)

    def col_copy(src, slot, to, i):
        return pltpu.make_async_remote_copy(
            src_ref=src, dst_ref=parts_ref.at[slot], send_sem=s4.at[i], recv_sem=r4.at[i],
            device_id={"cols": to}, device_id_type=MESH)

    if ncols == 4:
        across = lax.rem(mycol + 2, 4)
        beside = mycol + 1 - 2 * lax.rem(mycol, 2)
        corner = lax.rem(beside + 2, 4)
        first = col_copy(part_own, mycol, across, 0)
        first.start()
        second = col_copy(part_own, mycol, beside, 1)
        second.start()
        parts_ref[mycol] = part_own[...]
        own_ref[...] = jnp.transpose(values)[:width]
        col_copy(part_own, across, across, 0).wait_recv()
        third = col_copy(parts_ref.at[across], across, beside, 2)
        third.start()
        col_copy(part_own, beside, beside, 1).wait_recv()
        col_copy(part_own, corner, beside, 2).wait_recv()
        col_sends = (first, second, third)
    else:
        col_sends = tuple(
            col_copy(part_own, mycol, lax.rem(mycol + o, ncols), o) for o in range(1, ncols))
        for send in col_sends:
            send.start()
        parts_ref[mycol] = part_own[...]
        own_ref[...] = jnp.transpose(values)[:width]
        for o in range(1, ncols):
            came = lax.rem(mycol - o + ncols, ncols)
            col_copy(part_own, came, came, o).wait_recv()

    for bufs in ((req_out, req_in, s0, r0), (pick_out, pick_in, s1, r1),
                 (con_out, con_in, s2, r2), (mov_out, mov_in, s3, r3)):
        _each(n, lambda o, bufs=bufs: copy(*bufs, o).wait_send())
    for send in col_sends:
        send.wait_send()


def _small_inverse(p):
    m = len(p)
    if m == 1:
        return [[1.0 / p[0][0]]]
    if m == 2:
        inv = 1.0 / (p[0][0] * p[1][1] - p[0][1] * p[1][0])
        return [[p[1][1] * inv, -p[0][1] * inv], [-p[1][0] * inv, p[0][0] * inv]]
    h = m // 2

    def mul(a, b):
        return [
            [functools.reduce(jnp.add, [a[i][k] * b[k][j] for k in range(len(b))])
             for j in range(len(b[0]))]
            for i in range(len(a))
        ]

    a = [row[:h] for row in p[:h]]
    b = [row[h:] for row in p[:h]]
    c = [row[:h] for row in p[h:]]
    d = [row[h:] for row in p[h:]]
    ai = _small_inverse(a)
    cai = mul(c, ai)
    aib = mul(ai, b)
    caib = mul(cai, b)
    si = _small_inverse([[d[i][j] - caib[i][j] for j in range(h)] for i in range(h)])
    aibsi = mul(aib, si)
    sicai = mul(si, cai)
    corr = mul(aibsi, cai)
    top = [[ai[i][j] + corr[i][j] for j in range(h)] + [-aibsi[i][j] for j in range(h)]
           for i in range(h)]
    low = [[-sicai[i][j] for j in range(h)] + list(si[i]) for i in range(h)]
    return top + low


def _spd_inverse(gram, step):
    order = gram.shape[0]
    tiles = [gram[i : i + 8] for i in range(0, order, 8)]
    lane = _iota((8, order), 1)
    sub = _iota((8, order), 0)
    lane1 = _iota((1, order), 1)
    for k in range(0, order, step):
        at, off = k // 8, k % 8
        cols = [[jnp.broadcast_to(t[:, k + j : k + j + 1], (8, order)) for j in range(step)]
                for t in tiles]
        pivot = [[cols[at][j][off + i : off + i + 1] for j in range(step)] for i in range(step)]
        binv = _small_inverse(pivot)
        rows = [
            jnp.where((lane1 >= k) & (lane1 < k + step), (lane1 == k + i).astype(F32),
                      tiles[at][off + i : off + i + 1])
            for i in range(step)
        ]
        fresh = [functools.reduce(jnp.add, [binv[i][j] * rows[j] for j in range(step)])
                 for i in range(step)]
        inside = (lane >= k) & (lane < k + step)
        for x in range(len(tiles)):
            t = jnp.where(inside, 0.0, tiles[x])
            for j in range(step):
                t = t - cols[x][j] * fresh[j]
            if x == at:
                for i in range(step):
                    t = jnp.where(sub == off + i, fresh[i], t)
            tiles[x] = t
    return jnp.concatenate(tiles, axis=0)


def _dot3(a, b, dims):
    ah, al = _split2(a)
    bh, bl = _split2(b)
    return _dot(ah, bh, dims) + (_dot(ah, bl, dims) + _dot(al, bh, dims))


LIMIT = 64.0
SETTLED = 1e-5


def _solve_limits():
    limits = []
    for steps in range(4, 9):
        low, high = 1.0, 1e6
        for _ in range(100):
            mid = (low * high) ** 0.5
            rho = (mid - 1.0) / (mid + 1.0)
            for _ in range(steps):
                rho = rho * rho / (2.0 - rho * rho)
            low, high = (mid, high) if rho <= SETTLED else (low, mid)
        limits.append(low)
        if low >= LIMIT:
            break
    return limits


def _left(a):
    return jnp.concatenate(_split2(a), axis=1)


def _right(b):
    both = jnp.concatenate(_split2(b), axis=1)
    return jnp.concatenate([both, both], axis=0)


def _product(left, right):
    both = _dot(left, right)
    half = both.shape[1] // 2
    return both[:, :half] + both[:, half:]


def _narrow(rho):
    scale = 1.0 / (2.0 - rho * rho)
    return 2.0 * scale, rho * rho * scale


def _settling_solve(cross, gram, top):
    order = gram.shape[0]
    bound = jnp.max(top)
    eye = (_iota((order, order), 0) == _iota((order, order), 1)).astype(F32)
    limits = _solve_limits()
    count = 2 + functools.reduce(
        jnp.add, [(bound > limit).astype(jnp.int32) for limit in limits[:-1]])
    inv = 1.0 / (top + 1.0)
    scale, rho = _narrow((top - 1.0) * inv)
    first = 2.0 * inv
    x = (first * scale) * (2.0 * eye - first * gram)
    gram_left = _left(gram)

    def step(_, carry):
        x, rho = carry
        scale, rho = _narrow(rho)
        rest = scale * (2.0 * eye - _product(gram_left, _right(x)))
        return _product(_left(x), _right(rest)), rho

    cross_left = _left(jnp.transpose(cross))
    for _ in range(2):
        x, rho = step(0, (x, rho))
    x, rho = lax.fori_loop(2, count, step, (x, rho))
    right = _right(x)
    scale, rho = _narrow(rho)
    rest = scale * (2.0 * eye - _product(gram_left, right))
    return _product(_left(_product(cross_left, right)), _right(rest))


def leaf_kernel(parts_ref, own_ref, pickt_ref, pivots_ref, fwd_ref, trn_ref, interp_ref):
    ncols = parts_ref.shape[0]
    half = fwd_ref.shape[0]
    fwd_ref[...] = own_ref[:half]
    trn_ref[...] = own_ref[half:]
    cross, diag = 0.0, 0.0
    for c in range(ncols):
        code = parts_ref[c].astype(jnp.int32).astype(F32)
        tail = code[RANK:]
        cross = cross + code[:RANK] * (jnp.exp2(tail[:1]) * (1.0 / QMAX))
        diag = diag + tail[2:3] * (jnp.exp2(tail[1:2]) * (1.0 / QMAX))
    cross = cross + pickt_ref[...].astype(F32) * diag
    pick = (_iota((LEAF, RANK), 0) == pivots_ref[...]).astype(F32).astype(BF16)
    eye = (_iota((RANK, RANK), 0) == _iota((RANK, RANK), 1)).astype(F32)
    hi, lo = _split2(cross)
    gram = _dot(hi, pick) + _dot(lo, pick) + eye
    top = jnp.max(jnp.sum(jnp.abs(gram), axis=1, keepdims=True), axis=0, keepdims=True)
    settles = jnp.max(top) <= LIMIT

    @pl.when(settles)
    def _():
        interp_ref[...] = _settling_solve(cross, gram, top)

    @pl.when(jnp.logical_not(settles))
    def _():
        interp_ref[...] = _dot3(jnp.transpose(cross), _spd_inverse(gram, STEP), ((1,), (0,)))


def per_device(n, ncols, right_sample, left_sample, updates, pattern, targets, cluster_pos, pivots):
    children, block, _ = updates.shape
    rows_loc, half = right_sample.shape
    width = 2 * half
    lanes = _up(width + 2, 128)
    cap = _up(max(2, 3 * children * block // (2 * n)), 16)
    group = _up(rows_loc // n, 16)
    vmem = pl.BlockSpec(memory_space=pltpu.VMEM)
    smem = pl.BlockSpec(memory_space=pltpu.SMEM)
    i16 = jnp.int16
    parts, own, pickt = pl.pallas_call(
        functools.partial(moving_kernel, n, ncols, width, cap, group),
        out_shape=(
            jax.ShapeDtypeStruct((ncols, RANK + 16, LEAF), i16),
            jax.ShapeDtypeStruct((width, rows_loc), F32),
            jax.ShapeDtypeStruct((RANK, LEAF), BF16),
        ),
        in_specs=[vmem, vmem, vmem, smem, vmem, vmem, vmem],
        out_specs=(vmem, vmem, vmem),
        scratch_shapes=[
            pltpu.VMEM((rows_loc, lanes), BF16),
            pltpu.VMEM((n, 1, _up(cap, 128)), jnp.int32),
            pltpu.VMEM((n, 1, _up(cap, 128)), jnp.int32),
            pltpu.VMEM((n, rows_loc, cap), BF16),
            pltpu.VMEM((n, _packed(cap, lanes, width), 128), BF16),
            pltpu.VMEM((n, _packed(cap, lanes, width), 128), BF16),
            pltpu.VMEM((children * block, lanes), F32),
            pltpu.VMEM((n * cap, children * block), BF16),
            pltpu.VMEM((n, children * block, cap), BF16),
            pltpu.VMEM(updates.shape, BF16),
            pltpu.VMEM(updates.shape, BF16),
            pltpu.VMEM((n, _packed(cap, lanes, width), 128), i16),
            pltpu.VMEM((n, _packed(cap, lanes, width), 128), i16),
            pltpu.VMEM((n, _packed(group, lanes, width), 128), i16),
            pltpu.VMEM((n, _packed(group, lanes, width), 128), i16),
            pltpu.VMEM((RANK + 16, LEAF), i16),
        ]
        + [pltpu.SemaphoreType.DMA((n,))] * 8
        + [pltpu.SemaphoreType.DMA((ncols,))] * 2,
        compiler_params=pltpu.CompilerParams(collective_id=0, has_side_effects=True),
        name="moving",
    )(right_sample.T, left_sample.T, updates, pattern, targets.reshape(1, -1), cluster_pos.reshape(1, -1), pivots)
    forward, transposed, interp = pl.pallas_call(
        leaf_kernel,
        out_shape=(
            jax.ShapeDtypeStruct((half, rows_loc), F32),
            jax.ShapeDtypeStruct((half, rows_loc), F32),
            jax.ShapeDtypeStruct((rows_loc, RANK), F32),
        ),
        in_specs=[vmem] * 4,
        out_specs=(vmem, vmem, vmem),
        name="leaf",
    )(parts, own, pickt, pivots)
    return forward.T, transposed.T, interp


def solution(mesh):
    sizes = dict(mesh.shape)
    return jax.shard_map(
        functools.partial(per_device, sizes["rows"], sizes["cols"]),
        mesh=mesh,
        in_specs=(
            P("rows", "cols"),
            P("rows", "cols"),
            P("rows", None, None),
            P("rows", None, None),
            P("rows", None),
            P("rows"),
            P("rows", None),
        ),
        out_specs=(P("rows", "cols"), P("rows", "cols"), P("rows", None)),
        check_vma=False,
    )
```

profile of v0, /device:TPU:0, one launch (start us, length us, event | category | flops | bytes accessed | tf_op | source)
XLA Modules:
  0.0 43.7 jit_solution(2525559121400028090)
XLA Ops:
  0.6 39.1 %moving.1 = (s16[4,144,256]{2,1,0:T(8,128)(2,1)}, f32[160,256]{1,0:T(8,128)}, bf16[128,256]{1,0:T(8,128)(2,1)}) custom-call(bf16[80,256]{1,0:T(8,128)(2,1)} %bitcast.5, bf16[80,256]{1,0:T(8,128)(2,1)} %bitcast.6, bf16[1,512,512]{2,1,0:T(8,128)(2,1)} %updates_ref.1, s32[1,4,4]{2,1,0:T(4,128)} %pattern_ref.1, s32[1,512]{1,0:T(1,128)} %targets_ref.1, ...), custom_call_target="tpu_custom_call" | custom-call | tf_op jit(solution)/shard_map/moving/pallas_call | solution.py:536
  39.7 4.0 %leaf.1 = (f32[80,256]{1,0:T(8,128)}, f32[80,256]{1,0:T(8,128)}, f32[256,128]{1,0:T(8,128)}) custom-call(s16[4,144,256]{2,1,0:T(8,128)(2,1)} %get-tuple-element.9.parts_ref, f32[160,256]{1,0:T(8,128)} %get-tuple-element.10.own_ref, bf16[128,256]{1,0:T(8,128)(2,1)} %get-tuple-element.11.pickt_ref, s32[1,128]{1,0:T(1,128)} %pivots_ref.3), custom_call_target="tpu_custom_call" | custom-call | tf_op jit(solution)/shard_map/leaf/pallas_call | solution.py:568
where the time goes:
time: 43.8 us; the launch traced here: 43.7 us
  Pallas kernels  43 us (98%)
  between operations  0.64 us (1%)
    pallas_call x1, Pallas kernels, per_device(): pl.pallas_call(functools.partial(moving_kernel, n, ncols, width, cap, gro...  39.1 us
    pallas_call x1, Pallas kernels, per_device(): pl.pallas_call(leaf_kernel, out_shape=(jax.ShapeDtypeStruct((half, rows_l...  3.97 us

commit v1 on v0

--- a/solution.py
+++ b/solution.py
@@ -140,11 +140,22 @@
 
 def moving_kernel(
     n, ncols, width, cap, group,
-    right_ref, left_ref, updates_ref, pattern_ref, targets_ref, pos_ref, pivots_ref,
-    parts_ref, own_ref, pickt_ref,
+    right_hbm, left_hbm, updates_hbm, pattern_hbm, targets_hbm, pos_hbm, pivots_hbm,
+    parts_hbm, own_hbm, pickt_hbm,
     both_ref, req_out, req_in, hot_ref, pick_out, pick_in, gather_ref, sel_ref, selt_ref, masked_ref, masked_t_ref, con_out, con_in, mov_out, mov_in, part_own,
     s0, r0, s1, r1, s2, r2, s3, r3, s4, r4,
+    targets_ref, pos_ref, pivots_ref, right_ref, left_ref, pattern_ref, updates_ref, loaded,
+    parts_ref, own_ref, pickt_ref, stored,
 ):
+    loads = [
+        pltpu.make_async_copy(src, dst, loaded.at[i])
+        for i, (src, dst) in enumerate((
+            (targets_hbm, targets_ref), (pos_hbm, pos_ref), (pivots_hbm, pivots_ref),
+            (right_hbm, right_ref), (left_hbm, left_ref), (pattern_hbm, pattern_ref),
+            (updates_hbm, updates_ref)))
+    ]
+    for load in loads:
+        load.start()
     me = lax.axis_index("rows")
     mycol = lax.axis_index("cols")
     rows_loc, lanes = both_ref.shape
@@ -178,6 +189,7 @@
 
     half = width // 2
     sides = ((right_ref, 0), (left_ref, half))
+    loads[0].wait()
     slot, local = _positions(targets_ref[...], n, rows_loc, cap)
     digits = jnp.where(
         _iota((16, total), 0) < 8, jnp.bitwise_and(local, 255), jnp.right_shift(local, 8))
@@ -193,8 +205,12 @@
     pl.semaphore_wait(barrier, n - 1 + ncols - 1)
     _each(n, lambda o: copy(req_out, req_in, s0, r0, o).start(), far=True)
     make_request(me, req_in)
+    for load in loads[1:]:
+        load.wait()
     chosen = _iota((rows_loc, RANK), 0) == pivots_ref[...]
     pickt_ref[...] = jnp.transpose(chosen.astype(F32)).astype(BF16)
+    keep_pickt = pltpu.make_async_copy(pickt_ref, pickt_hbm, stored.at[ncols + 1])
+    keep_pickt.start()
 
     both_ref[...] = functools.reduce(jnp.add, [
         _dot(ref[...],
@@ -316,6 +332,11 @@
     part = _dot(shi, hi, NT) + (_dot(shi, lo, NT) + _dot(slo, hi, NT))
     part_own[...] = _encode_part(part * (1.0 / (2.0 * K)), pickt)
 
+    keep_own = pltpu.make_async_copy(own_ref, own_hbm, stored.at[ncols])
+
+    def keep_part(slot):
+        return pltpu.make_async_copy(parts_ref.at[slot], parts_hbm.at[slot], stored.at[slot])
+
     def col_copy(src, slot, to, i):
         return pltpu.make_async_remote_copy(
             src_ref=src, dst_ref=parts_ref.at[slot], send_sem=s4.at[i], recv_sem=r4.at[i],
@@ -331,11 +352,16 @@
         second.start()
         parts_ref[mycol] = part_own[...]
         own_ref[...] = jnp.transpose(values)[:width]
+        keep_own.start()
         col_copy(part_own, across, across, 0).wait_recv()
         third = col_copy(parts_ref.at[across], across, beside, 2)
         third.start()
+        keep_part(mycol).start()
+        keep_part(across).start()
         col_copy(part_own, beside, beside, 1).wait_recv()
+        keep_part(beside).start()
         col_copy(part_own, corner, beside, 2).wait_recv()
+        keep_part(corner).start()
         col_sends = (first, second, third)
     else:
         col_sends = tuple(
@@ -344,15 +370,22 @@
             send.start()
         parts_ref[mycol] = part_own[...]
         own_ref[...] = jnp.transpose(values)[:width]
+        keep_own.start()
         for o in range(1, ncols):
             came = lax.rem(mycol - o + ncols, ncols)
             col_copy(part_own, came, came, o).wait_recv()
+            keep_part(came).start()
+        keep_part(mycol).start()
 
     for bufs in ((req_out, req_in, s0, r0), (pick_out, pick_in, s1, r1),
                  (con_out, con_in, s2, r2), (mov_out, mov_in, s3, r3)):
         _each(n, lambda o, bufs=bufs: copy(*bufs, o).wait_send())
     for send in col_sends:
         send.wait_send()
+    for slot in range(ncols):
+        keep_part(slot).wait()
+    keep_own.wait()
+    keep_pickt.wait()
 
 
 def _small_inverse(p):
@@ -531,7 +564,7 @@
     cap = _up(max(2, 3 * children * block // (2 * n)), 16)
     group = _up(rows_loc // n, 16)
     vmem = pl.BlockSpec(memory_space=pltpu.VMEM)
-    smem = pl.BlockSpec(memory_space=pltpu.SMEM)
+    hbm = pl.BlockSpec(memory_space=pltpu.HBM)
     i16 = jnp.int16
     parts, own, pickt = pl.pallas_call(
         functools.partial(moving_kernel, n, ncols, width, cap, group),
@@ -540,8 +573,8 @@
             jax.ShapeDtypeStruct((width, rows_loc), F32),
             jax.ShapeDtypeStruct((RANK, LEAF), BF16),
         ),
-        in_specs=[vmem, vmem, vmem, smem, vmem, vmem, vmem],
-        out_specs=(vmem, vmem, vmem),
+        in_specs=[hbm] * 7,
+        out_specs=(hbm, hbm, hbm),
         scratch_shapes=[
             pltpu.VMEM((rows_loc, lanes), BF16),
             pltpu.VMEM((n, 1, _up(cap, 128)), jnp.int32),
@@ -561,7 +594,21 @@
             pltpu.VMEM((RANK + 16, LEAF), i16),
         ]
         + [pltpu.SemaphoreType.DMA((n,))] * 8
-        + [pltpu.SemaphoreType.DMA((ncols,))] * 2,
+        + [pltpu.SemaphoreType.DMA((ncols,))] * 2
+        + [
+            pltpu.VMEM((1, children * block), jnp.int32),
+            pltpu.VMEM((1, rows_loc), jnp.int32),
+            pltpu.VMEM(pivots.shape, jnp.int32),
+            pltpu.VMEM((half, rows_loc), BF16),
+            pltpu.VMEM((half, rows_loc), BF16),
+            pltpu.SMEM(pattern.shape, jnp.int32),
+            pltpu.VMEM(updates.shape, BF16),
+            pltpu.SemaphoreType.DMA((7,)),
+            pltpu.VMEM((ncols, RANK + 16, LEAF), i16),
+            pltpu.VMEM((width, rows_loc), F32),
+            pltpu.VMEM((RANK, LEAF), BF16),
+            pltpu.SemaphoreType.DMA((ncols + 2,)),
+        ],
         compiler_params=pltpu.CompilerParams(collective_id=0, has_side_effects=True),
         name="moving",
     )(right_sample.T, left_sample.T, updates, pattern, targets.reshape(1, -1), cluster_pos.reshape(1, -1), pivots)

time: 43.8 us -> 42.3 us (0.966); the launches traced: 43.7 us -> 41.5 us
  Pallas kernels: 43 us -> 40.8 us
    pallas_call x1, Pallas kernels: 39.1 us -> 37.2 us  [per_device(): pl.pallas_call(functools.partial(moving_kernel, n, ncols, width, cap, gro...]
where the time goes in v1:
time: 42.3 us; the launch traced here: 41.5 us
  Pallas kernels  40.8 us (96%)
  between operations  0.64 us (2%)
    pallas_call x1, Pallas kernels, per_device(): pl.pallas_call(functools.partial(moving_kernel, n, ncols, width, cap, gro...  37.2 us
    pallas_call x1, Pallas kernels, per_device(): pl.pallas_call(leaf_kernel, out_shape=(jax.ShapeDtypeStruct((half, rows_l...  3.61 us

profile of v1, /device:TPU:0, one launch (start us, length us, event | category | flops | bytes accessed | tf_op | source)
XLA Modules:
  0.0 41.5 jit_solution(16691700319216325319)
XLA Ops:
  0.6 37.2 %moving.1 = (s16[4,144,256]{2,1,0:T(8,128)(2,1)}, f32[160,256]{1,0:T(8,128)}, bf16[128,256]{1,0:T(8,128)(2,1)}) custom-call(bf16[80,256]{1,0:T(8,128)(2,1)} %bitcast.5, bf16[80,256]{1,0:T(8,128)(2,1)} %bitcast.6, bf16[1,512,512]{2,1,0:T(8,128)(2,1)} %updates_hbm.1, s32[1,4,4]{2,1,0:T(4,128)} %pattern_hbm.1, s32[1,512]{1,0:T(1,128)} %targets_hbm.1, ...), custom_call_target="tpu_custom_call" | custom-call | tf_op jit(solution)/shard_map/moving/pallas_call | solution.py:569
  37.9 3.6 %leaf.1 = (f32[80,256]{1,0:T(8,128)}, f32[80,256]{1,0:T(8,128)}, f32[256,128]{1,0:T(8,128)}) custom-call(s16[4,144,256]{2,1,0:T(8,128)(2,1)} %get-tuple-element.9.parts_ref, f32[160,256]{1,0:T(8,128)} %get-tuple-element.10.own_ref, bf16[128,256]{1,0:T(8,128)(2,1)} %get-tuple-element.11.pickt_ref, s32[1,128]{1,0:T(1,128)} %pivots_ref.1), custom_call_target="tpu_custom_call" | custom-call | tf_op jit(solution)/shard_map/leaf/pallas_call | solution.py:615
